TPU v7x, 128 devices: a whole 4x4x4 slice. The times are simulated.
128 devices in a mesh: pipe: 4 (over x), seq: 32 (over z, y, core).
Axes of the slice: x: 4, y: 4, z: 4, core: 2. Of those that a mesh axis runs over, the one named last changes fastest.
Arguments:
- query_rows: bfloat16 [4, 4096, 1536], P('pipe', 'seq'), may hold values from -6 to 6
- key_rows: bfloat16 [4, 4096, 1536], P('pipe', 'seq'), may hold values from -6 to 6
- value_rows: bfloat16 [4, 4096, 1536], P('pipe', 'seq'), may hold values from -6 to 6
- query_weight: bfloat16 [4, 1536, 1536], P('pipe'), may hold values from -0.15625 to 0.15625
- key_weight: bfloat16 [4, 1536, 1536], P('pipe'), may hold values from -0.15625 to 0.15625
- value_weight: bfloat16 [4, 1536, 1536], P('pipe'), may hold values from -0.15625 to 0.15625
- out_weight: bfloat16 [4, 1536, 1536], P('pipe'), may hold values from -0.15625 to 0.15625
- upstream: bfloat16 [4096, 1536], P('seq'), may hold values from -6 to 6
- window: int32 [32, 12, 2], replicated, may hold values from 0 to 1, as said below
Outputs:
- gradients: bfloat16 [4, 4096, 1536], P('pipe', 'seq')
Inputs may be any that keep to these rules, and one draw needn't show every extreme that they name: window[i, h, 0] is 0 where i % 4 == 3, and window[i, h, 1] is 0 where i % 4 == 2.
All inputs are finite; a program needn't handle non-finite values.
Results may differ from a plain program's by a relative error of at most 0.02.
Values may be sent and summed in bfloat16 or wider, within the bound.
A program may use at most 128 MiB of HBM per device.

v0:
```python
import jax
import jax.numpy as jnp
from jax import lax
from jax.sharding import PartitionSpec as P

HEADS = 12
HEAD_DIM = 128
TILE = 128


def extended_2(cells, sides, width):
    for axis, dim in sides:
        count = lax.axis_size(axis)
        ends = count - 1
        head = lax.slice_in_dim(cells, 0, width, axis=dim)
        tail = lax.slice_in_dim(cells, cells.shape[dim] - width, cells.shape[dim], axis=dim)
        cells = jnp.concatenate(
            [
                lax.ppermute(tail, axis, [(i, (i + 1) % count) for i in range(ends)]),
                cells,
                lax.ppermute(head, axis, [((i + 1) % count, i) for i in range(ends)]),
            ],
            axis=dim,
        )
    return cells


def from_behind(value, axis, steps):
    count = lax.axis_size(axis)
    leading, last = (max(0, -steps), min(count, count - steps))
    return lax.ppermute(value, axis, [(source, source + steps) for source in range(leading, last)])


def contract_last(first_operand, second_operand):
    return lax.dot_general(
        first_operand, second_operand, (((1,), (1,)), ((), ())), preferred_element_type=jnp.float32
    )


def attend(queries, grads_out, key_blocks, value_blocks, keep_mask, scaling):
    scores = scaling * jnp.einsum(
        "tqhd,tkhd->thqk", queries, key_blocks, preferred_element_type=jnp.float32
    )
    scores = jnp.where(keep_mask, scores, -jnp.inf)
    row_max = jnp.max(scores, axis=-1, keepdims=True)
    log_total = row_max + jnp.log(jnp.sum(jnp.exp(scores - row_max), axis=-1, keepdims=True))
    weights = jnp.exp(scores - log_total)
    weight_change = jnp.einsum(
        "tqhd,tkhd->thqk", grads_out, value_blocks, preferred_element_type=jnp.float32
    )
    row_delta = jnp.sum(weights * weight_change, axis=-1, keepdims=True)
    score_change = (weights * (weight_change - row_delta)).astype(jnp.bfloat16)
    return (log_total, row_delta, weights.astype(jnp.bfloat16), score_change)


def body(
    query_rows,
    key_rows,
    value_rows,
    query_weight,
    key_weight,
    value_weight,
    out_weight,
    upstream,
    window,
):
    sections = lax.axis_size("pipe")
    position = lax.axis_index("pipe")
    seq_index = lax.axis_index("seq")
    row_count = query_rows.shape[1]
    feature_count = query_rows.shape[2]
    tile_count = row_count // TILE
    model_width = out_weight.shape[2]
    scaling = HEAD_DIM ** (-0.5)
    tile_shape = (tile_count, TILE, HEADS, HEAD_DIM)
    queries = query_rows[0].reshape(tile_shape)
    query_matrix = query_weight[0]
    key_matrix = key_weight[0]
    value_matrix = value_weight[0]
    out_matrix = out_weight[0]
    padded_window = jnp.pad(window, ((1, 1), (0, 0), (0, 0)))
    local_window = (
        lax.dynamic_slice_in_dim(padded_window, seq_index * tile_count, tile_count + 2, 0) > 0
    )
    own_window = local_window[1 : tile_count + 1]
    middle_ones = jnp.ones((tile_count, HEADS, TILE), dtype=bool)
    keep_query = jnp.concatenate(
        [
            jnp.repeat(own_window[:, :, 0:1], TILE, axis=2),
            middle_ones,
            jnp.repeat(own_window[:, :, 1:2], TILE, axis=2),
        ],
        axis=2,
    )[:, :, None, :]
    paired = jnp.stack([key_rows[0], value_rows[0]], 0)
    extended = extended_2(paired, (("seq", 1),), TILE)
    ext_tiles = extended.reshape(2, tile_count + 2, TILE, HEADS, HEAD_DIM)
    blocks = jnp.concatenate(
        [
            ext_tiles[:, 0:tile_count],
            ext_tiles[:, 1 : tile_count + 1],
            ext_tiles[:, 2 : tile_count + 2],
        ],
        axis=2,
    )
    key_blocks = blocks[0]
    value_blocks = blocks[1]

    def make_out(incoming):
        return contract_last(incoming, out_matrix).astype(jnp.bfloat16)

    def project(incoming, query_gradient, key_gradient, value_gradient):
        total = incoming.astype(jnp.float32) + contract_last(query_gradient, query_matrix)
        total = (
            total
            + contract_last(key_gradient, key_matrix)
            + contract_last(value_gradient, value_matrix)
        )
        return total.astype(jnp.bfloat16)

    def query_pass(incoming):
        d_out = make_out(incoming)
        out_tiles = d_out.reshape(tile_shape)
        log_total, row_delta, weights_low, score_change = attend(
            queries, out_tiles, key_blocks, value_blocks, keep_query, scaling
        )
        query_gradient = (
            scaling
            * jnp.einsum(
                "thqk,tkhd->tqhd", score_change, key_blocks, preferred_element_type=jnp.float32
            )
        ).astype(jnp.bfloat16)
        return (
            d_out,
            out_tiles,
            log_total,
            row_delta,
            weights_low,
            score_change,
            query_gradient.reshape(row_count, feature_count),
        )

    def spare_back(operand):
        return jnp.zeros((row_count, model_width), jnp.bfloat16)

    result = jnp.zeros((row_count, model_width), jnp.bfloat16)
    incoming = upstream
    for step_index in range(sections):
        active = position == sections - 1 - step_index

        def front_returned(operand):
            d_out, out_tiles, log_total, row_delta, weights_low, score_change, query_gradient = (
                query_pass(operand)
            )
            key_part = scaling * jnp.einsum(
                "thqk,tqhd->tkhd", score_change, queries, preferred_element_type=jnp.float32
            )
            value_part = jnp.einsum(
                "thqk,tqhd->tkhd", weights_low, out_tiles, preferred_element_type=jnp.float32
            )
            partials = jnp.stack([key_part, value_part], 0).reshape(
                2, tile_count, 3, TILE, feature_count
            )
            summed = jnp.zeros((2, tile_count + 2, TILE, feature_count), jnp.float32)
            for offset in range(3):
                summed = summed.at[:, offset : offset + tile_count].add(partials[:, :, offset])
            return (query_gradient, summed)

        def spare_front_returned(operand):
            return (
                jnp.zeros((row_count, feature_count), jnp.bfloat16),
                jnp.zeros((2, tile_count + 2, TILE, feature_count), jnp.float32),
            )

        query_gradient, summed = lax.cond(active, front_returned, spare_front_returned, incoming)
        from_next = from_behind(summed[:, 0].astype(jnp.bfloat16), "seq", -1).astype(jnp.float32)
        from_prev = from_behind(summed[:, tile_count + 1].astype(jnp.bfloat16), "seq", 1).astype(
            jnp.float32
        )

        def back_returned(operand):
            carried, query_gradient, summed, from_next, from_prev = operand
            own_sums = summed[:, 1 : tile_count + 1]
            own_sums = own_sums.at[:, tile_count - 1].add(from_next)
            own_sums = own_sums.at[:, 0].add(from_prev)
            own_sums = own_sums.astype(jnp.bfloat16).reshape(2, row_count, feature_count)
            return project(carried, query_gradient, own_sums[0], own_sums[1])

        finished = lax.cond(
            active,
            back_returned,
            spare_back,
            (incoming, query_gradient, summed, from_next, from_prev),
        )
        result = jnp.where(active, finished, result)
        if step_index < sections - 1:
            incoming = from_behind(finished, "pipe", -1)
    return result[None]


def solution(mesh):
    in_specs = (
        P("pipe", "seq", None),
        P("pipe", "seq", None),
        P("pipe", "seq", None),
        P("pipe", None, None),
        P("pipe", None, None),
        P("pipe", None, None),
        P("pipe", None, None),
        P("seq", None),
        P(),
    )
    out_specs = P("pipe", "seq", None)
    return jax.shard_map(body, mesh=mesh, in_specs=in_specs, out_specs=out_specs, check_vma=False)
```

profile of v0, /device:TPU:57, one launch (start us, length us, event | category | flops | bytes accessed | tf_op | source)
XLA Modules:
  0.0 329.6 jit_solution(3800161639839907413)
XLA Ops:
  4.7 5.1 %collective-permute-start = (bf16[2,128,1536]{2,1,0:T(8,128)(2,1)S(1)}, bf16[2,128,1536]{2,1,0:T(8,128)(2,1)S(1)}, u32[]{:S(2)}, u32[]{:S(2)}) collective-permute-start(bf16[2,128,1536]{2,1,0:T(8,128)(2,1)S(1)} %constant_dynamic-update-slice_fusion), channel_id=1, source_target_pairs={{0,1},{1,2},{2,3},{3,4},{4,5},{5,6},{6,7},{7,8},{8,9},{9,10},{10,1... | collective-permute-start | bytes 2359304 | tf_op jit(solution)/shard_map/ppermute | solution.py:19
  11.9 5.6 %collective-permute-done.1 = bf16[2,128,1536]{2,1,0:T(8,128)(2,1)S(1)} collective-permute-done((bf16[2,128,1536]{2,1,0:T(8,128)(2,1)S(1)}, bf16[2,128,1536]{2,1,0:T(8,128)(2,1)S(1)}, u32[]{:S(2)}, u32[]{:S(2)}) %collective-permute-start.1) | collective-permute-done | bytes 786464 | tf_op jit(solution)/shard_map/ppermute | solution.py:21
  20.2 5.5 %reshape.1081 = bf16[2,3,128,12,128]{4,3,2,1,0:T(8,128)(2,1)} reshape(bf16[2,384,1536]{2,1,0:T(8,128)(2,1)} %pad_maximum_fusion.5) | data formatting | bytes 4718592 | tf_op jit(solution)/shard_map/reshape | solution.py:97
  31.3 3.7 %conditional.8 = (bf16[128,1536]{0,1:T(8,128)(2,1)}, f32[2,3,128,1536]{3,2,0,1:T(8,128)}) conditional(s32[]{:T(128)} %convert_element_type.203, () %tuple.145, (pred[1,12,1,384]{3,1,2,0:T(8,128)(4,1)S(1)}, bf16[1,128,12,128]{1,3,2,0:T(8,128)(2,1)S(1)}, bf16[1,384,12,128]{3,1,2,0:T(8,128)(2,1)S(1)}, bf16[128,1536]{1,0:T(8,128)(2,1)S(1)}, ...), branch_computations={%region_0.1_spmd, %region_1.5_spmd} | conditional | flops 1374680064 | bytes 101147288 | solution.py:175
  37.8 6.5 %collective-permute-start.3 = (bf16[2,128,1536]{2,1,0:T(8,128)(2,1)S(1)}, bf16[2,128,1536]{2,1,0:T(8,128)(2,1)S(1)}, u32[]{:S(2)}, u32[]{:S(2)}) collective-permute-start(bf16[2,128,1536]{2,1,0:T(8,128)(2,1)S(1)} %get-tuple-element.558), channel_id=1, source_target_pairs={{0,1},{1,2},{2,3},{3,4},{4,5},{5,6},{6,7},{7,8},{8,9},{9,10},{10,1... | collective-permute-start | bytes 2359304 | tf_op jit(solution)/shard_map/ppermute | solution.py:31
  46.2 7.0 %collective-permute-done.3 = bf16[2,128,1536]{2,1,0:T(8,128)(2,1)S(1)} collective-permute-done((bf16[2,128,1536]{2,1,0:T(8,128)(2,1)S(1)}, bf16[2,128,1536]{2,1,0:T(8,128)(2,1)S(1)}, u32[]{:S(2)}, u32[]{:S(2)}) %collective-permute-start.3) | collective-permute-done | bytes 786464 | tf_op jit(solution)/shard_map/ppermute | solution.py:31
  54.5 5.2 %collective-permute-done.2 = bf16[2,128,1536]{2,1,0:T(8,128)(2,1)S(1)} collective-permute-done((bf16[2,128,1536]{2,1,0:T(8,128)(2,1)S(1)}, bf16[2,128,1536]{2,1,0:T(8,128)(2,1)S(1)}, u32[]{:S(2)}, u32[]{:S(2)}) %collective-permute-start.2) | collective-permute-done | bytes 786464 | tf_op jit(solution)/shard_map/ppermute | solution.py:31
  62.7 7.3 %collective-permute-done.4 = bf16[128,1536]{1,0:T(8,128)(2,1)} collective-permute-done((bf16[128,1536]{1,0:T(8,128)(2,1)S(1)}, bf16[128,1536]{1,0:T(8,128)(2,1)}, u32[]{:S(2)}, u32[]{:S(2)}) %collective-permute-start.4) | collective-permute-done | bytes 393248 | tf_op jit(solution)/shard_map/ppermute | solution.py:31
  70.0 4.0 %conditional.10 = (bf16[128,1536]{0,1:T(8,128)(2,1)}, f32[2,3,128,1536]{3,2,0,1:T(8,128)}) conditional(s32[]{:T(128)} %convert_element_type.202, () %tuple.148, (pred[1,12,1,384]{3,1,2,0:T(8,128)(4,1)S(1)}, bf16[1,128,12,128]{1,3,2,0:T(8,128)(2,1)S(1)}, bf16[1,384,12,128]{3,1,2,0:T(8,128)(2,1)S(1)}, bf16[128,1536]{1,0:T(8,128)(2,1)}, ...), branch_computations={%region_7.8_spmd, %region_8.12_spmd} | conditional | flops 1374680064 | bytes 101147288 | solution.py:175
  81.6 7.0 %collective-permute-done.6 = bf16[2,128,1536]{2,1,0:T(8,128)(2,1)S(1)} collective-permute-done((bf16[2,128,1536]{2,1,0:T(8,128)(2,1)S(1)}, bf16[2,128,1536]{2,1,0:T(8,128)(2,1)S(1)}, u32[]{:S(2)}, u32[]{:S(2)}) %collective-permute-start.6) | collective-permute-done | bytes 786464 | tf_op jit(solution)/shard_map/ppermute | solution.py:31
  89.9 5.2 %collective-permute-done.5 = bf16[2,128,1536]{2,1,0:T(8,128)(2,1)S(1)} collective-permute-done((bf16[2,128,1536]{2,1,0:T(8,128)(2,1)S(1)}, bf16[2,128,1536]{2,1,0:T(8,128)(2,1)S(1)}, u32[]{:S(2)}, u32[]{:S(2)}) %collective-permute-start.5) | collective-permute-done | bytes 786464 | tf_op jit(solution)/shard_map/ppermute | solution.py:31
  98.0 7.5 %collective-permute-done.7 = bf16[128,1536]{1,0:T(8,128)(2,1)} collective-permute-done((bf16[128,1536]{1,0:T(8,128)(2,1)S(1)}, bf16[128,1536]{1,0:T(8,128)(2,1)}, u32[]{:S(2)}, u32[]{:S(2)}) %collective-permute-start.7) | collective-permute-done | bytes 393248 | tf_op jit(solution)/shard_map/ppermute | solution.py:31
  105.5 3.5 %conditional.12 = (bf16[128,1536]{0,1:T(8,128)(2,1)}, f32[2,3,128,1536]{3,2,0,1:T(8,128)}) conditional(s32[]{:T(128)} %convert_element_type.201, () %tuple.151, (pred[1,12,1,384]{3,1,2,0:T(8,128)(4,1)S(1)}, bf16[1,128,12,128]{1,3,2,0:T(8,128)(2,1)S(1)}, bf16[1,384,12,128]{3,1,2,0:T(8,128)(2,1)S(1)}, bf16[128,1536]{1,0:T(8,128)(2,1)}, ...), branch_computations={%region_14.15_spmd, %region_15.19_spmd} | conditional | flops 1374680064 | bytes 101147288 | solution.py:175
  116.8 7.0 %collective-permute-done.9 = bf16[2,128,1536]{2,1,0:T(8,128)(2,1)S(1)} collective-permute-done((bf16[2,128,1536]{2,1,0:T(8,128)(2,1)S(1)}, bf16[2,128,1536]{2,1,0:T(8,128)(2,1)S(1)}, u32[]{:S(2)}, u32[]{:S(2)}) %collective-permute-start.9) | collective-permute-done | bytes 786464 | tf_op jit(solution)/shard_map/ppermute | solution.py:31
  125.2 5.2 %collective-permute-done.8 = bf16[2,128,1536]{2,1,0:T(8,128)(2,1)S(1)} collective-permute-done((bf16[2,128,1536]{2,1,0:T(8,128)(2,1)S(1)}, bf16[2,128,1536]{2,1,0:T(8,128)(2,1)S(1)}, u32[]{:S(2)}, u32[]{:S(2)}) %collective-permute-start.8) | collective-permute-done | bytes 786464 | tf_op jit(solution)/shard_map/ppermute | solution.py:31
  133.3 128.0 %collective-permute-done.10 = bf16[128,1536]{1,0:T(8,128)(2,1)S(1)} collective-permute-done((bf16[128,1536]{1,0:T(8,128)(2,1)S(1)}, bf16[128,1536]{1,0:T(8,128)(2,1)S(1)}, u32[]{:S(2)}, u32[]{:S(2)}) %collective-permute-start.10) | collective-permute-done | bytes 393248 | tf_op jit(solution)/shard_map/ppermute | solution.py:31
  262.0 35.6 %conditional.14 = (bf16[128,1536]{0,1:T(8,128)(2,1)S(1)}, f32[2,3,128,1536]{3,2,0,1:T(8,128)}) conditional(s32[]{:T(128)} %convert_element_type.200, () %tuple.154, (pred[1,12,1,384]{3,1,2,0:T(8,128)(4,1)S(1)}, bf16[1,128,12,128]{1,3,2,0:T(8,128)(2,1)S(1)}, bf16[1,384,12,128]{3,1,2,0:T(8,128)(2,1)S(1)}, bf16[128,1536]{1,0:T(8,128)(2,1)S(1)}, ...), branch_computations={%region_21.22_spmd, %region_22.26_spmd} | conditional | flops 1374680064 | bytes 101147240 | solution.py:175
  262.0 4.0 %convolution_convert_fusion.3 = bf16[128,1536]{1,0:T(8,128)(2,1)S(1)} fusion(bf16[128,1536]{1,0:T(8,128)(2,1)S(1)} %get-tuple-element.414, bf16[1536,1536]{1,0:T(8,128)(2,1)} %get-tuple-element.415), kind=kOutput, calls=%fused_computation.151 | convolution fusion | flops 604176384 | bytes 5505024 | tf_op jit(solution)/shard_map/cond/branch_1_fun/dot_general | solution.py:35
  272.9 4.6 %reshape.1085 = f32[1,1,3,128,1536]{3,2,4,1,0:T(4,128)} reshape(f32[1,384,12,128]{1,3,2,0:T(8,128)} %convolution_bitcast_fusion.3) | data formatting | bytes 4718592 | tf_op jit(solution)/shard_map/cond/branch_1_fun/stack | solution.py:161
  285.4 4.0 %stack.35 = f32[1,1,3,128,1536]{4,3,2,1,0:T(8,128)} reshape(f32[1,384,12,128]{3,2,1,0:T(8,128)} %copy.77) | data formatting | bytes 4718592 | tf_op jit(solution)/shard_map/cond/branch_1_fun/stack | solution.py:161
  300.4 3.4 %collective-permute-start.12 = (bf16[2,128,1536]{2,1,0:T(8,128)(2,1)S(1)}, bf16[2,128,1536]{2,1,0:T(8,128)(2,1)S(1)}, u32[]{:S(2)}, u32[]{:S(2)}) collective-permute-start(bf16[2,128,1536]{2,1,0:T(8,128)(2,1)S(1)} %get-tuple-element.552), channel_id=1, source_target_pairs={{0,1},{1,2},{2,3},{3,4},{4,5},{5,6},{6,7},{7,8},{8,9},{9,10},{10,1... | collective-permute-start | bytes 2359304 | tf_op jit(solution)/shard_map/ppermute | solution.py:31
  305.7 7.0 %collective-permute-done.12 = bf16[2,128,1536]{2,1,0:T(8,128)(2,1)S(1)} collective-permute-done((bf16[2,128,1536]{2,1,0:T(8,128)(2,1)S(1)}, bf16[2,128,1536]{2,1,0:T(8,128)(2,1)S(1)}, u32[]{:S(2)}, u32[]{:S(2)}) %collective-permute-start.12) | collective-permute-done | bytes 786464 | tf_op jit(solution)/shard_map/ppermute | solution.py:31
  312.8 6.3 %collective-permute-done.11 = bf16[2,128,1536]{2,1,0:T(8,128)(2,1)S(1)} collective-permute-done((bf16[2,128,1536]{2,1,0:T(8,128)(2,1)S(1)}, bf16[2,128,1536]{2,1,0:T(8,128)(2,1)S(1)}, u32[]{:S(2)}, u32[]{:S(2)}) %collective-permute-start.11) | collective-permute-done | bytes 786464 | tf_op jit(solution)/shard_map/ppermute | solution.py:31
  319.3 9.2 %conditional.15 = (bf16[128,1536]{1,0:T(8,128)(2,1)S(1)}) conditional(s32[]{:T(128)} %convert_element_type.200, () %tuple.141, (bf16[128,1536]{1,0:T(8,128)(2,1)}, bf16[128,1536]{0,1:T(8,128)(2,1)S(1)}, bf16[1536,1536]{1,0:T(8,128)(2,1)}, f32[2,3,128,1536]{3,2,0,1:T(8,128)}, f32[2,128,1536]{2,1,0:T(8,128)S(1)}, ...), branch_computations={%region_26.27_spmd, %region_27.28_spmd} | conditional | flops 1814102016 | bytes 82968696 | solution.py:189
  (119 shorter events, 97.0 us)
Async XLA Ops:
  0.0 11.0 %copy-start.44 = (s32[32,12,2]{0,2,1:T(2,128)S(1)}, s32[32,12,2]{0,2,1:T(2,128)}, u32[]{:S(2)}) copy-start(s32[32,12,2]{0,2,1:T(2,128)} %param.73) | copy-start | bytes 9220
  2.1 15.4 %collective-permute-start.1 = (bf16[2,128,1536]{2,1,0:T(8,128)(2,1)S(1)}, bf16[2,128,1536]{2,1,0:T(8,128)(2,1)S(1)}, u32[]{:S(2)}, u32[]{:S(2)}) collective-permute-start(bf16[2,128,1536]{2,1,0:T(8,128)(2,1)S(1)} %constant_dynamic-update-slice_fusion), channel_id=1, source_target_pairs={{1,0},{2,1},{3,2},{4,3},{5,4},{6,5},{7,6},{8,7},{9,8},{10,9},{11,1... | collective-permute-start | bytes 2359304 | tf_op jit(solution)/shard_map/ppermute | solution.py:21
  4.7 14.0 %collective-permute-start = (bf16[2,128,1536]{2,1,0:T(8,128)(2,1)S(1)}, bf16[2,128,1536]{2,1,0:T(8,128)(2,1)S(1)}, u32[]{:S(2)}, u32[]{:S(2)}) collective-permute-start(bf16[2,128,1536]{2,1,0:T(8,128)(2,1)S(1)} %constant_dynamic-update-slice_fusion), channel_id=1, source_target_pairs={{0,1},{1,2},{2,3},{3,4},{4,5},{5,6},{6,7},{7,8},{8,9},{9,10},{10,1... | collective-permute-start | bytes 2359304 | tf_op jit(solution)/shard_map/ppermute | solution.py:19
  11.0 20.3 %copy-start.16 = (bf16[1,128,1536]{1,2,0:T(8,128)(2,1)}, bf16[1,128,1536]{1,2,0:T(8,128)(2,1)S(1)}, u32[]{:S(2)}) copy-start(bf16[1,128,1536]{1,2,0:T(8,128)(2,1)S(1)} %copy.82) | copy-start | bytes 1179652
  37.8 15.4 %collective-permute-start.3 = (bf16[2,128,1536]{2,1,0:T(8,128)(2,1)S(1)}, bf16[2,128,1536]{2,1,0:T(8,128)(2,1)S(1)}, u32[]{:S(2)}, u32[]{:S(2)}) collective-permute-start(bf16[2,128,1536]{2,1,0:T(8,128)(2,1)S(1)} %get-tuple-element.558), channel_id=1, source_target_pairs={{0,1},{1,2},{2,3},{3,4},{4,5},{5,6},{6,7},{7,8},{8,9},{9,10},{10,1... | collective-permute-start | bytes 2359304 | tf_op jit(solution)/shard_map/ppermute | solution.py:31
  44.3 15.4 %collective-permute-start.2 = (bf16[2,128,1536]{2,1,0:T(8,128)(2,1)S(1)}, bf16[2,128,1536]{2,1,0:T(8,128)(2,1)S(1)}, u32[]{:S(2)}, u32[]{:S(2)}) collective-permute-start(bf16[2,128,1536]{2,1,0:T(8,128)(2,1)S(1)} %get-tuple-element.559), channel_id=1, source_target_pairs={{1,0},{2,1},{3,2},{4,3},{5,4},{6,5},{7,6},{8,7},{9,8},{10,9},{11,1... | collective-permute-start | bytes 2359304 | tf_op jit(solution)/shard_map/ppermute | solution.py:31
  59.7 10.3 %copy-start.24 = (bf16[1,384,12,128]{3,2,1,0:T(8,128)(2,1)S(1)}, bf16[1,384,12,128]{3,2,1,0:T(8,128)(2,1)}, u32[]{:S(2)}) copy-start(bf16[1,384,12,128]{3,2,1,0:T(8,128)(2,1)} %copy-done.23) | copy-start | bytes 3538948
  61.1 8.9 %copy-start.17 = (bf16[1,128,1536]{1,2,0:T(8,128)(2,1)S(1)}, bf16[1,128,1536]{1,2,0:T(8,128)(2,1)}, u32[]{:S(2)}) copy-start(bf16[1,128,1536]{1,2,0:T(8,128)(2,1)} %copy-done.16) | copy-start | bytes 1179652
  61.4 8.6 %copy-start.37 = (bf16[128,1536]{1,0:T(8,128)(2,1)}, bf16[128,1536]{1,0:T(8,128)(2,1)S(1)}, u32[]{:S(2)}) copy-start(bf16[128,1536]{1,0:T(8,128)(2,1)S(1)} %get-tuple-element.576) | copy-start | bytes 1179652
  61.4 8.6 %collective-permute-start.4 = (bf16[128,1536]{1,0:T(8,128)(2,1)S(1)}, bf16[128,1536]{1,0:T(8,128)(2,1)}, u32[]{:S(2)}, u32[]{:S(2)}) collective-permute-start(bf16[128,1536]{1,0:T(8,128)(2,1)S(1)} %get-tuple-element.576), channel_id=1, source_target_pairs={{32,0},{64,32},{96,64},{33,1},{65,33},{97,65},{34,2},{66,34},{98,6... | collective-permute-start | bytes 1179656 | tf_op jit(solution)/shard_map/ppermute | solution.py:31
  76.7 11.8 %collective-permute-start.6 = (bf16[2,128,1536]{2,1,0:T(8,128)(2,1)S(1)}, bf16[2,128,1536]{2,1,0:T(8,128)(2,1)S(1)}, u32[]{:S(2)}, u32[]{:S(2)}) collective-permute-start(bf16[2,128,1536]{2,1,0:T(8,128)(2,1)S(1)} %get-tuple-element.556), channel_id=1, source_target_pairs={{0,1},{1,2},{2,3},{3,4},{4,5},{5,6},{6,7},{7,8},{8,9},{9,10},{10,1... | collective-permute-start | bytes 2359304 | tf_op jit(solution)/shard_map/ppermute | solution.py:31
  79.6 15.4 %collective-permute-start.5 = (bf16[2,128,1536]{2,1,0:T(8,128)(2,1)S(1)}, bf16[2,128,1536]{2,1,0:T(8,128)(2,1)S(1)}, u32[]{:S(2)}, u32[]{:S(2)}) collective-permute-start(bf16[2,128,1536]{2,1,0:T(8,128)(2,1)S(1)} %get-tuple-element.557), channel_id=1, source_target_pairs={{1,0},{2,1},{3,2},{4,3},{5,4},{6,5},{7,6},{8,7},{9,8},{10,9},{11,1... | collective-permute-start | bytes 2359304 | tf_op jit(solution)/shard_map/ppermute | solution.py:31
  95.1 10.4 %copy-start.25 = (bf16[1,384,12,128]{3,2,1,0:T(8,128)(2,1)S(1)}, bf16[1,384,12,128]{3,2,1,0:T(8,128)(2,1)}, u32[]{:S(2)}) copy-start(bf16[1,384,12,128]{3,2,1,0:T(8,128)(2,1)} %copy-done.23) | copy-start | bytes 3538948
  96.5 9.0 %copy-start.18 = (bf16[1,128,1536]{1,2,0:T(8,128)(2,1)S(1)}, bf16[1,128,1536]{1,2,0:T(8,128)(2,1)}, u32[]{:S(2)}) copy-start(bf16[1,128,1536]{1,2,0:T(8,128)(2,1)} %copy-done.16) | copy-start | bytes 1179652
  96.5 9.0 %copy-start.38 = (bf16[128,1536]{1,0:T(8,128)(2,1)}, bf16[128,1536]{1,0:T(8,128)(2,1)S(1)}, u32[]{:S(2)}) copy-start(bf16[128,1536]{1,0:T(8,128)(2,1)S(1)} %get-tuple-element.577) | copy-start | bytes 1179652
  96.6 8.9 %collective-permute-start.7 = (bf16[128,1536]{1,0:T(8,128)(2,1)S(1)}, bf16[128,1536]{1,0:T(8,128)(2,1)}, u32[]{:S(2)}, u32[]{:S(2)}) collective-permute-start(bf16[128,1536]{1,0:T(8,128)(2,1)S(1)} %get-tuple-element.577), channel_id=1, source_target_pairs={{32,0},{64,32},{96,64},{33,1},{65,33},{97,65},{34,2},{66,34},{98,6... | collective-permute-start | bytes 1179656 | tf_op jit(solution)/shard_map/ppermute | solution.py:31
  111.8 12.0 %collective-permute-start.9 = (bf16[2,128,1536]{2,1,0:T(8,128)(2,1)S(1)}, bf16[2,128,1536]{2,1,0:T(8,128)(2,1)S(1)}, u32[]{:S(2)}, u32[]{:S(2)}) collective-permute-start(bf16[2,128,1536]{2,1,0:T(8,128)(2,1)S(1)} %get-tuple-element.554), channel_id=1, source_target_pairs={{0,1},{1,2},{2,3},{3,4},{4,5},{5,6},{6,7},{7,8},{8,9},{9,10},{10,1... | collective-permute-start | bytes 2359304 | tf_op jit(solution)/shard_map/ppermute | solution.py:31
  114.9 15.4 %collective-permute-start.8 = (bf16[2,128,1536]{2,1,0:T(8,128)(2,1)S(1)}, bf16[2,128,1536]{2,1,0:T(8,128)(2,1)S(1)}, u32[]{:S(2)}, u32[]{:S(2)}) collective-permute-start(bf16[2,128,1536]{2,1,0:T(8,128)(2,1)S(1)} %get-tuple-element.555), channel_id=1, source_target_pairs={{1,0},{2,1},{3,2},{4,3},{5,4},{6,5},{7,6},{8,7},{9,8},{10,9},{11,1... | collective-permute-start | bytes 2359304 | tf_op jit(solution)/shard_map/ppermute | solution.py:31
  131.7 129.5 %copy-start.19 = (bf16[1,128,1536]{1,2,0:T(8,128)(2,1)S(1)}, bf16[1,128,1536]{1,2,0:T(8,128)(2,1)}, u32[]{:S(2)}) copy-start(bf16[1,128,1536]{1,2,0:T(8,128)(2,1)} %copy-done.16) | copy-start | bytes 1179652
  131.9 129.3 %copy-start.39 = (bf16[128,1536]{1,0:T(8,128)(2,1)}, bf16[128,1536]{1,0:T(8,128)(2,1)S(1)}, u32[]{:S(2)}) copy-start(bf16[128,1536]{1,0:T(8,128)(2,1)S(1)} %get-tuple-element.578) | copy-start | bytes 1179652
  132.0 129.3 %collective-permute-start.10 = (bf16[128,1536]{1,0:T(8,128)(2,1)S(1)}, bf16[128,1536]{1,0:T(8,128)(2,1)S(1)}, u32[]{:S(2)}, u32[]{:S(2)}) collective-permute-start(bf16[128,1536]{1,0:T(8,128)(2,1)S(1)} %get-tuple-element.578), channel_id=1, source_target_pairs={{32,0},{64,32},{96,64},{33,1},{65,33},{97,65},{34,2},{66,34},{98,6... | collective-permute-start | bytes 1179656 | tf_op jit(solution)/shard_map/ppermute | solution.py:31
  300.4 12.3 %collective-permute-start.12 = (bf16[2,128,1536]{2,1,0:T(8,128)(2,1)S(1)}, bf16[2,128,1536]{2,1,0:T(8,128)(2,1)S(1)}, u32[]{:S(2)}, u32[]{:S(2)}) collective-permute-start(bf16[2,128,1536]{2,1,0:T(8,128)(2,1)S(1)} %get-tuple-element.552), channel_id=1, source_target_pairs={{0,1},{1,2},{2,3},{3,4},{4,5},{5,6},{6,7},{7,8},{8,9},{9,10},{10,1... | collective-permute-start | bytes 2359304 | tf_op jit(solution)/shard_map/ppermute | solution.py:31
  303.7 15.4 %collective-permute-start.11 = (bf16[2,128,1536]{2,1,0:T(8,128)(2,1)S(1)}, bf16[2,128,1536]{2,1,0:T(8,128)(2,1)S(1)}, u32[]{:S(2)}, u32[]{:S(2)}) collective-permute-start(bf16[2,128,1536]{2,1,0:T(8,128)(2,1)S(1)} %get-tuple-element.553), channel_id=1, source_target_pairs={{1,0},{2,1},{3,2},{4,3},{5,4},{6,5},{7,6},{8,7},{9,8},{10,9},{11,1... | collective-permute-start | bytes 2359304 | tf_op jit(solution)/shard_map/ppermute | solution.py:31
  319.4 2.9 copy-start.43
  (11 other events, 24.0 us)
where the time goes:
time: 334 us; the launch traced here: 330 us
  waiting for transfers between devices  199 us (60%)
  local copies, waits for them, and re-layouts  46.2 us (14%)
  starting transfers between devices  35.2 us (11%)
  other arithmetic  31.2 us (9%)
  matrix products  15.7 us (5%)
    ppermute x11, waiting for transfers between devices, from_behind(): lax.ppermute(value, axis, [(source, source + steps) for source in range(l...  193 us
    ppermute x11, starting transfers between devices, from_behind(): lax.ppermute(value, axis, [(source, source + steps) for source in range(l...  27.6 us
    another operation x3, local copies, waits for them, and re-layouts, front_returned(): jnp.stack([key_part, value_part], 0)  11.6 us
    another operation x9, local copies, waits for them, and re-layouts  10.7 us
    another operation x4, other arithmetic  10.5 us
    dot_general x4, matrix products, contract_last(): lax.dot_general(first_operand, second_operand, (((1,), (1,)), ((), ())),...  8.9 us
  transfers between devices with their start and end apart: 13, of which 13 were waited for; matrix products, arithmetic and copies ran while one was open for 2% of the time, Pallas kernels for 0%

commit v1 on v0

v1 whole, which is shorter than its diff:
```python
import functools

import jax
import jax.numpy as jnp
from jax import lax
from jax.experimental import pallas as pl
from jax.experimental.pallas import tpu as pltpu
from jax.sharding import PartitionSpec as P

HEAD_DIM = 128
COLUMN = 4
CHUNK = 256
MESH = pl.DeviceIdType.MESH
F32 = jnp.float32
BF16 = jnp.bfloat16
LOW = -1e30


def nt(a, b):
    return lax.dot_general(a, b, (((1,), (1,)), ((), ())), preferred_element_type=F32)


def nn(a, b):
    return lax.dot_general(a, b, (((1,), (0,)), ((), ())), preferred_element_type=F32)


def relay_kernel(
    sections, tiles, heads, tile,
    q_hbm, k_hbm, v_hbm, wq_hbm, wk_hbm, wv_hbm, wo_hbm, up_hbm, window_ref,
    out_ref,
    qx, kx, vx, wq, wk, wv, wo, inx, acc, dx, prob, prob_t, mean_v, lsx, dlt, grad, res, stat,
    load_sem, wsem, up_sem,
    kv_send, kv_recv, ls_send, ls_recv, hop_send, hop_recv, fwd_send, fwd_recv, dl_send, dl_recv,
):
    width = q_hbm.shape[2]
    model = up_hbm.shape[1]
    chunks = model // CHUNK
    scaling = HEAD_DIM ** (-0.5)
    stage = lax.axis_index("pipe")
    me = lax.axis_index("seq")
    has_left = jnp.logical_and(lax.rem(me, COLUMN) != COLUMN - 1, me > 0)
    has_right = jnp.logical_and(lax.rem(me, COLUMN) != COLUMN - 2, me < tiles - 1)
    is_first = stage == sections - 1
    sends_on = stage > 0
    own = pl.ds(tile, tile)
    low_rows = pl.ds(0, tile)
    high_rows = pl.ds(2 * tile, tile)
    sides = (
        (0, has_left, {"seq": me - 1}, high_rows),
        (1, has_right, {"seq": me + 1}, low_rows),
    )
    here = ((0, has_left, low_rows), (1, has_right, high_rows))

    barrier = pltpu.get_barrier_semaphore()
    for condition, target in (
        (has_left, {"seq": me - 1}),
        (has_right, {"seq": me + 1}),
        (sends_on, {"pipe": stage - 1}),
        (jnp.logical_not(is_first), {"pipe": stage + 1}),
    ):
        @pl.when(condition)
        def _(target=target):
            pl.semaphore_signal(barrier, inc=1, device_id=target, device_id_type=MESH)

    own_loads = [
        pltpu.make_async_copy(source.at[0], target.at[own], load_sem.at[n])
        for n, (source, target) in enumerate(((k_hbm, kx), (v_hbm, vx), (q_hbm, qx)))
    ]
    for copy in own_loads:
        copy.start()
    weight_loads = [
        pltpu.make_async_copy(source.at[0], target, wsem.at[n])
        for n, (source, target) in enumerate(((wo_hbm, wo), (wq_hbm, wq), (wk_hbm, wk), (wv_hbm, wv)))
    ]
    for n in range(chunks):
        @pl.when(is_first)
        def _(n=n):
            pltpu.make_async_copy(
                up_hbm.at[:, pl.ds(n * CHUNK, CHUNK)], inx.at[n, own], up_sem.at[n]
            ).start()
    for copy in weight_loads:
        copy.start()

    for side, present, rows in here:
        @pl.when(jnp.logical_not(present))
        def _(side=side, rows=rows):
            for ref in (kx, vx, qx):
                ref[rows, :] = jnp.zeros((tile, width), BF16)
            for n in range(chunks):
                inx[n, rows, :] = jnp.zeros((tile, CHUNK), BF16)
            lsx[:, rows] = jnp.zeros((16, tile), F32)
            dlt[:, rows] = jnp.zeros((16, tile), F32)

    one = lambda flag: jnp.where(flag, 1, 0)
    pl.semaphore_wait(
        barrier,
        one(has_left) + one(has_right) + one(sends_on) + one(jnp.logical_not(is_first)),
    )

    def exchange(ordinal, side, target, rows, source, into):
        return pltpu.make_async_remote_copy(
            src_ref=source, dst_ref=into.at[rows],
            send_sem=kv_send.at[ordinal, side], recv_sem=kv_recv.at[ordinal, side],
            device_id=target, device_id_type=MESH,
        )

    statics = ((0, k_hbm, kx), (1, v_hbm, vx), (2, q_hbm, qx))
    for ordinal, source, into in statics:
        for side, present, target, rows in sides:
            @pl.when(present)
            def _(ordinal=ordinal, side=side, target=target, rows=rows, source=source, into=into):
                exchange(ordinal, side, target, rows, source.at[0], into).start()

    def wait_static(ordinal, into):
        for side, present, rows in here:
            @pl.when(present)
            def _(side=side, rows=rows):
                pltpu.make_async_remote_copy(
                    src_ref=into.at[own], dst_ref=into.at[rows],
                    send_sem=kv_send.at[ordinal, 1 - side], recv_sem=kv_recv.at[ordinal, 1 - side],
                    device_id={"seq": me}, device_id_type=MESH,
                ).wait_recv()

    def small_copy(source, into, rows, side, send, recv, target):
        return pltpu.make_async_remote_copy(
            src_ref=source, dst_ref=into.at[:, rows],
            send_sem=send.at[side], recv_sem=recv.at[side],
            device_id=target, device_id_type=MESH,
        )

    def wait_small(into, send, recv):
        for side, present, rows in here:
            @pl.when(present)
            def _(side=side, rows=rows):
                small_copy(into.at[:, own], into, rows, 1 - side, send, recv, {"seq": me}).wait_recv()

    lanes = lax.broadcasted_iota(jnp.int32, (tile, 128), 1)

    def head_cols(h):
        return pl.ds(pl.multiple_of(h * HEAD_DIM, HEAD_DIM), HEAD_DIM)

    def flag(index, h, which):
        return window_ref[index, pl.ds(h, 1), which:which + 1]

    before = jnp.maximum(me - 1, 0)
    after = jnp.minimum(me + 1, tiles - 1)

    for copy in own_loads[:2]:
        copy.wait()
    wait_static(0, kx)
    wait_static(1, vx)

    def forward_head(h, table):
        cols = head_cols(h)
        scores = scaling * nt(qx[own, cols], kx[:, cols])
        left = jnp.where(flag(me, h, 0) > 0, scores[:, :tile], LOW)
        right = jnp.where(flag(me, h, 1) > 0, scores[:, 2 * tile:], LOW)
        scores = jnp.concatenate([left, scores[:, tile:2 * tile], right], axis=1)
        top = jnp.max(scores, axis=1, keepdims=True)
        powers = jnp.exp(scores - top)
        total = jnp.sum(powers, axis=1, keepdims=True)
        weights = powers * (1.0 / total)
        prob[h] = weights
        high = weights.astype(BF16)
        rest = (weights - high.astype(F32)).astype(BF16)
        values = vx[:, cols]
        mean_v[:, cols] = nn(high, values) + nn(rest, values)
        return jnp.where(lanes == h, top + jnp.log(total), table)

    own_loads[2].wait()
    table = lax.fori_loop(0, heads, forward_head, jnp.zeros((tile, 128), F32))
    stat[...] = table.T
    lsx[:, own] = stat[0:16, :]
    for side, present, target, rows in sides:
        @pl.when(present)
        def _(side=side, target=target, rows=rows):
            small_copy(lsx.at[:, own], lsx, rows, side, ls_send, ls_recv, target).start()

    def forward_chunk(n, side, target, rows):
        return pltpu.make_async_remote_copy(
            src_ref=inx.at[n, own], dst_ref=inx.at[n, rows],
            send_sem=fwd_send.at[n, side], recv_sem=fwd_recv.at[n, side],
            device_id=target, device_id_type=MESH,
        )

    def forward_all(n):
        for side, present, target, rows in sides:
            @pl.when(present)
            def _(side=side, target=target, rows=rows):
                forward_chunk(n, side, target, rows).start()

    @pl.when(is_first)
    def _():
        for n in range(chunks):
            pltpu.make_async_copy(
                up_hbm.at[:, pl.ds(n * CHUNK, CHUNK)], inx.at[n, own], up_sem.at[n]
            ).wait()
            forward_all(n)

    acc[...] = jnp.zeros_like(acc)
    wait_static(2, qx)
    wait_small(lsx, ls_send, ls_recv)

    def transposed_head(h, carry):
        cols = head_cols(h)
        scores = scaling * nt(kx[own, cols], qx[:, cols]) - lsx[pl.ds(h, 1), :]
        left_flag = jnp.logical_and(flag(before, h, 1) > 0, me > 0)
        right_flag = jnp.logical_and(flag(after, h, 0) > 0, me < tiles - 1)
        left = jnp.where(left_flag, scores[:, :tile], LOW)
        right = jnp.where(right_flag, scores[:, 2 * tile:], LOW)
        scores = jnp.concatenate([left, scores[:, tile:2 * tile], right], axis=1)
        prob_t[h] = jnp.exp(scores)
        return carry

    lax.fori_loop(0, heads, transposed_head, 0)
    weight_loads[0].wait()

    def hop_copy(n):
        return pltpu.make_async_remote_copy(
            src_ref=res.at[n], dst_ref=inx.at[n, own],
            send_sem=hop_send.at[n], recv_sem=hop_recv.at[n],
            device_id={"pipe": stage - 1}, device_id_type=MESH,
        )

    def wait_forwarded(n):
        for side, present, rows in here:
            @pl.when(present)
            def _(side=side, rows=rows):
                forward_chunk(n, 1 - side, {"seq": me}, rows).wait_recv()

    def accumulate(n):
        k_cols = pl.ds(n * CHUNK, CHUNK)
        last = n == chunks - 1

        @pl.loop(0, width // CHUNK)
        def _(m):
            out_cols = pl.ds(pl.multiple_of(m * CHUNK, CHUNK), CHUNK)
            part = acc[:, out_cols] + nt(inx[n], wo[out_cols, k_cols])
            if last:
                dx[:, out_cols] = part.astype(BF16)
            else:
                acc[:, out_cols] = part

    for n in range(chunks):
        @pl.when(jnp.logical_not(is_first))
        def _(n=n):
            hop_copy(n).wait_recv()
            forward_all(n)
        if n > 0:
            wait_forwarded(n - 1)
            accumulate(n - 1)
    wait_forwarded(chunks - 1)
    accumulate(chunks - 1)

    def delta_head(h, table):
        cols = head_cols(h)
        delta = jnp.sum(dx[own, cols].astype(F32) * mean_v[:, cols], axis=1, keepdims=True)
        return jnp.where(lanes == h, delta, table)

    stat[...] = lax.fori_loop(0, heads, delta_head, jnp.zeros((tile, 128), F32)).T
    dlt[:, own] = stat[0:16, :]
    for side, present, target, rows in sides:
        @pl.when(present)
        def _(side=side, target=target, rows=rows):
            small_copy(dlt.at[:, own], dlt, rows, side, dl_send, dl_recv, target).start()

    def query_head(h, carry):
        cols = head_cols(h)
        d_own = dx[own, cols]
        delta = jnp.sum(d_own.astype(F32) * mean_v[:, cols], axis=1, keepdims=True)
        change = (prob[h] * (nt(d_own, vx[:, cols]) - delta)).astype(BF16)
        grad[0, :, cols] = (scaling * nn(change, kx[:, cols])).astype(BF16)
        grad[2, :, cols] = nn(prob_t[h].astype(BF16), dx[:, cols]).astype(BF16)
        return carry

    lax.fori_loop(0, heads, query_head, 0)
    wait_small(dlt, dl_send, dl_recv)

    def key_head(h, carry):
        cols = head_cols(h)
        change = (prob_t[h] * (nt(vx[own, cols], dx[:, cols]) - dlt[pl.ds(h, 1), :])).astype(BF16)
        grad[1, :, cols] = (scaling * nn(change, qx[:, cols])).astype(BF16)
        return carry

    lax.fori_loop(0, heads, key_head, 0)
    for copy in weight_loads[1:]:
        copy.wait()

    for n in range(chunks):
        rows = pl.ds(n * CHUNK, CHUNK)
        total = inx[n, own, :].astype(F32) + nt(grad[0], wq[rows, :])
        total = total + nt(grad[1], wk[rows, :]) + nt(grad[2], wv[rows, :])
        total = total.astype(BF16)
        res[n] = total

        @pl.when(sends_on)
        def _(n=n):
            hop_copy(n).start()
        out_ref[0, :, rows] = total

    for side, present, target, rows in sides:
        @pl.when(present)
        def _(side=side, target=target, rows=rows):
            for ordinal, source, into in statics:
                exchange(ordinal, side, target, rows, source.at[0], into).wait_send()
            small_copy(lsx.at[:, own], lsx, rows, side, ls_send, ls_recv, target).wait_send()
            small_copy(dlt.at[:, own], dlt, rows, side, dl_send, dl_recv, target).wait_send()
            for n in range(chunks):
                forward_chunk(n, side, target, rows).wait_send()

    @pl.when(sends_on)
    def _():
        for n in range(chunks):
            hop_copy(n).wait_send()


def body(q, k, v, wq, wk, wv, wo, upstream, window):
    sections = lax.axis_size("pipe")
    tiles = window.shape[0]
    heads = window.shape[1]
    tile = q.shape[1]
    width = q.shape[2]
    model = upstream.shape[1]
    chunks = model // CHUNK
    hbm = pl.BlockSpec(memory_space=pl.ANY)
    vmem = pl.BlockSpec(memory_space=pltpu.VMEM)
    dma = pltpu.SemaphoreType.DMA
    return pl.pallas_call(
        functools.partial(relay_kernel, sections, tiles, heads, tile),
        out_shape=jax.ShapeDtypeStruct((1, tile, model), BF16),
        in_specs=[hbm] * 8 + [vmem],
        out_specs=vmem,
        scratch_shapes=[
            pltpu.VMEM((3 * tile, width), BF16),
            pltpu.VMEM((3 * tile, width), BF16),
            pltpu.VMEM((3 * tile, width), BF16),
            pltpu.VMEM((model, width), BF16),
            pltpu.VMEM((model, width), BF16),
            pltpu.VMEM((model, width), BF16),
            pltpu.VMEM((width, model), BF16),
            pltpu.VMEM((chunks, 3 * tile, CHUNK), BF16),
            pltpu.VMEM((3 * tile, width), F32),
            pltpu.VMEM((3 * tile, width), BF16),
            pltpu.VMEM((heads, tile, 3 * tile), F32),
            pltpu.VMEM((heads, tile, 3 * tile), F32),
            pltpu.VMEM((tile, width), F32),
            pltpu.VMEM((16, 3 * tile), F32),
            pltpu.VMEM((16, 3 * tile), F32),
            pltpu.VMEM((3, tile, width), BF16),
            pltpu.VMEM((chunks, tile, CHUNK), BF16),
            pltpu.VMEM((128, tile), F32),
            dma((3,)), dma((4,)), dma((chunks,)),
            dma((3, 2)), dma((3, 2)), dma((2,)), dma((2,)),
            dma((chunks,)), dma((chunks,)), dma((chunks, 2)), dma((chunks, 2)),
            dma((2,)), dma((2,)),
        ],
        compiler_params=pltpu.CompilerParams(
            collective_id=0, has_side_effects=True, vmem_limit_bytes=60 * 1024 * 1024
        ),
    )(q, k, v, wq, wk, wv, wo, upstream, window)


def solution(mesh):
    in_specs = (
        P("pipe", "seq", None),
        P("pipe", "seq", None),
        P("pipe", "seq", None),
        P("pipe", None, None),
        P("pipe", None, None),
        P("pipe", None, None),
        P("pipe", None, None),
        P("seq", None),
        P(),
    )
    out_specs = P("pipe", "seq", None)
    return jax.shard_map(body, mesh=mesh, in_specs=in_specs, out_specs=out_specs, check_vma=False)
```

time: 334 us -> 156 us (0.47); the launches traced: 330 us -> 156 us
  waiting for transfers between devices: 199 us -> 0 us
  Pallas kernels: 0 us -> 152 us
  local copies, waits for them, and re-layouts: 46.2 us -> 3.35 us
  starting transfers between devices: 35.2 us -> 0 us
  other arithmetic: 31.2 us -> 0 us
  matrix products: 15.7 us -> 0 us
    ppermute x13 -> x0, waiting for transfers between devices: 199 us -> none  [the longest x11 193 us: from_behind(): lax.ppermute(value, axis, [(source, source + steps) for source in range(l...]
    pallas_call x0 -> x1, Pallas kernels: none -> 152 us  [body(): pl.pallas_call(functools.partial(relay_kernel, sections, tiles, heads, ti...]
    ppermute x13 -> x0, starting transfers between devices: 35.2 us -> none  [the longest x11 27.6 us: from_behind(): lax.ppermute(value, axis, [(source, source + steps) for source in range(l...]
    another operation x13 -> x0, local copies, waits for them, and re-layouts: 23.2 us -> none  [the longest x3 11.6 us: front_returned(): jnp.stack([key_part, value_part], 0)]
    dot_general x9 -> x0, matrix products: 15.7 us -> none  [the longest x4 8.9 us: contract_last(): lax.dot_general(first_operand, second_operand, (((1,), (1,)), ((), ())),...]
    convert_element_type x10 -> x0, other arithmetic: 11.3 us -> none  [the longest x4 4.45 us: body(): from_behind(summed[:, 0].astype(jnp.bfloat16), 'seq', -1)]
    another operation x4 -> x0, other arithmetic: 10.5 us -> none
    reshape x3 -> x0, local copies, waits for them, and re-layouts: 5.61 us -> none  [the longest x1 5.47 us: body(): ext_tiles = extended.reshape(2, tile_count + 2, TILE, HEADS, HEAD_DIM)]
  transfers between devices with their start and end apart: 13 -> 0, of which waited for: 13 -> 0; matrix products, arithmetic and copies ran while one was open for 2% -> 0% of each run, Pallas kernels for 0% -> 0%
where the time goes in v1:
time: 156 us
  Pallas kernels  152 us (97%)
  local copies, waits for them, and re-layouts  3.35 us (2%)
    pallas_call x1, Pallas kernels, body(): pl.pallas_call(functools.partial(relay_kernel, sections, tiles, heads, ti...  152 us
    unnamed x2, local copies, waits for them, and re-layouts  3.35 us

profile of v1, /device:TPU:57, one launch (start us, length us, event | category | flops | bytes accessed | tf_op | source)
XLA Modules:
  0.0 155.8 jit_solution(4294600687883560109)
XLA Ops:
  0.0 1.6 %copy.10.window_ref = s32[32,12,2]{2,1,0:T(8,128)} copy(s32[32,12,2]{0,2,1:T(2,128)} %param.17) | data formatting | bytes 6144 | tf_op args[8]
  1.6 152.5 %shard_map.91 = bf16[1,128,1536]{2,1,0:T(8,128)(2,1)} custom-call(bf16[1,128,1536]{2,1,0:T(8,128)(2,1)} %q_hbm.1, bf16[1,128,1536]{2,1,0:T(8,128)(2,1)} %k_hbm.1, bf16[1,128,1536]{2,1,0:T(8,128)(2,1)} %v_hbm.1, bf16[1,1536,1536]{2,1,0:T(8,128)(2,1)} %wq_hbm.1, bf16[1,1536,1536]{2,1,0:T(8,128)(2,1)} %wk_hbm.1, bf16[1,1536,1536]{2,1,0:T(8,128)(2,1)} %wv_hbm.1, ...), custom_call_target="tpu_custom_call" | custom-call | tf_op jit(solution)/shard_map/pallas_call | solution.py:328
  154.1 1.8 %copy.12 = bf16[1,128,1536]{2,1,0:T(8,128)(2,1)} copy(bf16[1,128,1536]{2,1,0:T(8,128)(2,1)} %shard_map.91) | data formatting | bytes 786432

commit v2 on v1

--- a/solution.py
+++ b/solution.py
@@ -104,12 +104,39 @@
             device_id=target, device_id_type=MESH,
         )
 
+    def forward_chunk(n, side, target, rows):
+        return pltpu.make_async_remote_copy(
+            src_ref=inx.at[n, own], dst_ref=inx.at[n, rows],
+            send_sem=fwd_send.at[n, side], recv_sem=fwd_recv.at[n, side],
+            device_id=target, device_id_type=MESH,
+        )
+
+    def forward_all(n):
+        for side, present, target, rows in sides:
+            @pl.when(present)
+            def _(side=side, target=target, rows=rows):
+                forward_chunk(n, side, target, rows).start()
+
     statics = ((0, k_hbm, kx), (1, v_hbm, vx), (2, q_hbm, qx))
-    for ordinal, source, into in statics:
+
+    def start_static(ordinal, source, into):
         for side, present, target, rows in sides:
             @pl.when(present)
-            def _(ordinal=ordinal, side=side, target=target, rows=rows, source=source, into=into):
+            def _(side=side, target=target, rows=rows):
                 exchange(ordinal, side, target, rows, source.at[0], into).start()
+
+    start_static(*statics[0])
+    start_static(*statics[1])
+
+    @pl.when(is_first)
+    def _():
+        for n in range(chunks):
+            pltpu.make_async_copy(
+                up_hbm.at[:, pl.ds(n * CHUNK, CHUNK)], inx.at[n, own], up_sem.at[n]
+            ).wait()
+            forward_all(n)
+
+    start_static(*statics[2])
 
     def wait_static(ordinal, into):
         for side, present, rows in here:
@@ -137,6 +164,8 @@
     lanes = lax.broadcasted_iota(jnp.int32, (tile, 128), 1)
 
     def head_cols(h):
+        if isinstance(h, int):
+            return pl.ds(h * HEAD_DIM, HEAD_DIM)
         return pl.ds(pl.multiple_of(h * HEAD_DIM, HEAD_DIM), HEAD_DIM)
 
     def flag(index, h, which):
@@ -168,38 +197,13 @@
         return jnp.where(lanes == h, top + jnp.log(total), table)
 
     own_loads[2].wait()
-    table = lax.fori_loop(0, heads, forward_head, jnp.zeros((tile, 128), F32))
+    table = lax.fori_loop(0, heads, forward_head, jnp.zeros((tile, 128), F32), unroll=4)
     stat[...] = table.T
     lsx[:, own] = stat[0:16, :]
     for side, present, target, rows in sides:
         @pl.when(present)
         def _(side=side, target=target, rows=rows):
             small_copy(lsx.at[:, own], lsx, rows, side, ls_send, ls_recv, target).start()
-
-    def forward_chunk(n, side, target, rows):
-        return pltpu.make_async_remote_copy(
-            src_ref=inx.at[n, own], dst_ref=inx.at[n, rows],
-            send_sem=fwd_send.at[n, side], recv_sem=fwd_recv.at[n, side],
-            device_id=target, device_id_type=MESH,
-        )
-
-    def forward_all(n):
-        for side, present, target, rows in sides:
-            @pl.when(present)
-            def _(side=side, target=target, rows=rows):
-                forward_chunk(n, side, target, rows).start()
-
-    @pl.when(is_first)
-    def _():
-        for n in range(chunks):
-            pltpu.make_async_copy(
-                up_hbm.at[:, pl.ds(n * CHUNK, CHUNK)], inx.at[n, own], up_sem.at[n]
-            ).wait()
-            forward_all(n)
-
-    acc[...] = jnp.zeros_like(acc)
-    wait_static(2, qx)
-    wait_small(lsx, ls_send, ls_recv)
 
     def transposed_head(h, carry):
         cols = head_cols(h)
@@ -212,7 +216,12 @@
         prob_t[h] = jnp.exp(scores)
         return carry
 
-    lax.fori_loop(0, heads, transposed_head, 0)
+    def transposed_all():
+        wait_static(2, qx)
+        wait_small(lsx, ls_send, ls_recv)
+        lax.fori_loop(0, heads, transposed_head, 0, unroll=4)
+
+    pl.when(jnp.logical_not(is_first))(transposed_all)
     weight_loads[0].wait()
 
     def hop_copy(n):
@@ -232,10 +241,11 @@
         k_cols = pl.ds(n * CHUNK, CHUNK)
         last = n == chunks - 1
 
-        @pl.loop(0, width // CHUNK)
-        def _(m):
-            out_cols = pl.ds(pl.multiple_of(m * CHUNK, CHUNK), CHUNK)
-            part = acc[:, out_cols] + nt(inx[n], wo[out_cols, k_cols])
+        for m in range(width // CHUNK):
+            out_cols = pl.ds(m * CHUNK, CHUNK)
+            part = nt(inx[n], wo[out_cols, k_cols])
+            if n > 0:
+                part = part + acc[:, out_cols]
             if last:
                 dx[:, out_cols] = part.astype(BF16)
             else:
@@ -251,38 +261,42 @@
             accumulate(n - 1)
     wait_forwarded(chunks - 1)
     accumulate(chunks - 1)
+    pl.when(is_first)(transposed_all)
 
     def delta_head(h, table):
         cols = head_cols(h)
         delta = jnp.sum(dx[own, cols].astype(F32) * mean_v[:, cols], axis=1, keepdims=True)
         return jnp.where(lanes == h, delta, table)
 
-    stat[...] = lax.fori_loop(0, heads, delta_head, jnp.zeros((tile, 128), F32)).T
+    table = jnp.zeros((tile, 128), F32)
+    for h in range(heads):
+        table = delta_head(h, table)
+    stat[...] = table.T
     dlt[:, own] = stat[0:16, :]
     for side, present, target, rows in sides:
         @pl.when(present)
         def _(side=side, target=target, rows=rows):
             small_copy(dlt.at[:, own], dlt, rows, side, dl_send, dl_recv, target).start()
 
-    def query_head(h, carry):
+    def query_head(h):
         cols = head_cols(h)
         d_own = dx[own, cols]
         delta = jnp.sum(d_own.astype(F32) * mean_v[:, cols], axis=1, keepdims=True)
         change = (prob[h] * (nt(d_own, vx[:, cols]) - delta)).astype(BF16)
         grad[0, :, cols] = (scaling * nn(change, kx[:, cols])).astype(BF16)
         grad[2, :, cols] = nn(prob_t[h].astype(BF16), dx[:, cols]).astype(BF16)
-        return carry
-
-    lax.fori_loop(0, heads, query_head, 0)
+
+    for h in range(heads):
+        query_head(h)
     wait_small(dlt, dl_send, dl_recv)
 
-    def key_head(h, carry):
+    def key_head(h):
         cols = head_cols(h)
         change = (prob_t[h] * (nt(vx[own, cols], dx[:, cols]) - dlt[pl.ds(h, 1), :])).astype(BF16)
         grad[1, :, cols] = (scaling * nn(change, qx[:, cols])).astype(BF16)
-        return carry
-
-    lax.fori_loop(0, heads, key_head, 0)
+
+    for h in range(heads):
+        key_head(h)
     for copy in weight_loads[1:]:
         copy.wait()
 

time: 156 us -> 121 us (0.78); the launches traced: 156 us -> 119 us
  Pallas kernels: 152 us -> 116 us
    pallas_call x1, Pallas kernels: 152 us -> 116 us  [body(): pl.pallas_call(functools.partial(relay_kernel, sections, tiles, heads, ti...]
where the time goes in v2:
time: 121 us; the launch traced here: 119 us
  Pallas kernels  116 us (96%)
  local copies, waits for them, and re-layouts  3.35 us (3%)
    pallas_call x1, Pallas kernels, body(): pl.pallas_call(functools.partial(relay_kernel, sections, tiles, heads, ti...  116 us
    unnamed x2, local copies, waits for them, and re-layouts  3.35 us

profile of v2, /device:TPU:57, one launch (start us, length us, event | category | flops | bytes accessed | tf_op | source)
XLA Modules:
  0.0 119.1 jit_solution(5374922970967595134)
XLA Ops:
  0.0 1.6 %copy.10.window_ref = s32[32,12,2]{2,1,0:T(8,128)} copy(s32[32,12,2]{0,2,1:T(2,128)} %param.17) | data formatting | bytes 6144 | tf_op args[8]
  1.6 115.7 %shard_map.91 = bf16[1,128,1536]{2,1,0:T(8,128)(2,1)} custom-call(bf16[1,128,1536]{2,1,0:T(8,128)(2,1)} %q_hbm.1, bf16[1,128,1536]{2,1,0:T(8,128)(2,1)} %k_hbm.1, bf16[1,128,1536]{2,1,0:T(8,128)(2,1)} %v_hbm.1, bf16[1,1536,1536]{2,1,0:T(8,128)(2,1)} %wq_hbm.1, bf16[1,1536,1536]{2,1,0:T(8,128)(2,1)} %wk_hbm.1, bf16[1,1536,1536]{2,1,0:T(8,128)(2,1)} %wv_hbm.1, ...), custom_call_target="tpu_custom_call" | custom-call | tf_op jit(solution)/shard_map/pallas_call | solution.py:342
  117.3 1.8 %copy.12 = bf16[1,128,1536]{2,1,0:T(8,128)(2,1)} copy(bf16[1,128,1536]{2,1,0:T(8,128)(2,1)} %shard_map.91) | data formatting | bytes 786432

commit v3 on v2

--- a/solution.py
+++ b/solution.py
@@ -10,6 +10,7 @@
 HEAD_DIM = 128
 COLUMN = 4
 CHUNK = 256
+LAG = 2
 MESH = pl.DeviceIdType.MESH
 F32 = jnp.float32
 BF16 = jnp.bfloat16
@@ -237,31 +238,34 @@
             def _(side=side, rows=rows):
                 forward_chunk(n, 1 - side, {"seq": me}, rows).wait_recv()
 
-    def accumulate(n):
-        k_cols = pl.ds(n * CHUNK, CHUNK)
-        last = n == chunks - 1
-
+    def accumulate(n, row_sets):
+        rows_in = [inx[n, rows, :] for rows in row_sets]
+        incoming = rows_in[0] if len(rows_in) == 1 else jnp.concatenate(rows_in, axis=0)
         for m in range(width // CHUNK):
             out_cols = pl.ds(m * CHUNK, CHUNK)
-            part = nt(inx[n], wo[out_cols, k_cols])
-            if n > 0:
-                part = part + acc[:, out_cols]
-            if last:
-                dx[:, out_cols] = part.astype(BF16)
-            else:
-                acc[:, out_cols] = part
+            product = nt(incoming, wo[out_cols, pl.ds(n * CHUNK, CHUNK)])
+            for i, rows in enumerate(row_sets):
+                part = product[i * tile:(i + 1) * tile]
+                if n > 0:
+                    part = part + acc[rows, out_cols]
+                if n == chunks - 1:
+                    dx[rows, out_cols] = part.astype(BF16)
+                else:
+                    acc[rows, out_cols] = part
+
+    def accumulate_halo(n):
+        wait_forwarded(n)
+        accumulate(n, (low_rows, high_rows))
 
     for n in range(chunks):
+        if n >= LAG:
+            accumulate_halo(n - LAG)
+
         @pl.when(jnp.logical_not(is_first))
         def _(n=n):
             hop_copy(n).wait_recv()
             forward_all(n)
-        if n > 0:
-            wait_forwarded(n - 1)
-            accumulate(n - 1)
-    wait_forwarded(chunks - 1)
-    accumulate(chunks - 1)
-    pl.when(is_first)(transposed_all)
+        accumulate(n, (own,))
 
     def delta_head(h, table):
         cols = head_cols(h)
@@ -284,14 +288,17 @@
         delta = jnp.sum(d_own.astype(F32) * mean_v[:, cols], axis=1, keepdims=True)
         change = (prob[h] * (nt(d_own, vx[:, cols]) - delta)).astype(BF16)
         grad[0, :, cols] = (scaling * nn(change, kx[:, cols])).astype(BF16)
-        grad[2, :, cols] = nn(prob_t[h].astype(BF16), dx[:, cols]).astype(BF16)
 
     for h in range(heads):
         query_head(h)
+    for n in range(chunks - LAG, chunks):
+        accumulate_halo(n)
+    pl.when(is_first)(transposed_all)
     wait_small(dlt, dl_send, dl_recv)
 
     def key_head(h):
         cols = head_cols(h)
+        grad[2, :, cols] = nn(prob_t[h].astype(BF16), dx[:, cols]).astype(BF16)
         change = (prob_t[h] * (nt(vx[own, cols], dx[:, cols]) - dlt[pl.ds(h, 1), :])).astype(BF16)
         grad[1, :, cols] = (scaling * nn(change, qx[:, cols])).astype(BF16)
 

time: 121 us -> 109 us (0.901); the launches traced: 119 us -> 109 us
  Pallas kernels: 116 us -> 105 us
    pallas_call x1, Pallas kernels: 116 us -> 105 us  [body(): pl.pallas_call(functools.partial(relay_kernel, sections, tiles, heads, ti...]
where the time goes in v3:
time: 109 us
  Pallas kernels  105 us (96%)
  local copies, waits for them, and re-layouts  3.35 us (3%)
    pallas_call x1, Pallas kernels, body(): pl.pallas_call(functools.partial(relay_kernel, sections, tiles, heads, ti...  105 us
    unnamed x2, local copies, waits for them, and re-layouts  3.35 us

profile of v3, /device:TPU:57, one launch (start us, length us, event | category | flops | bytes accessed | tf_op | source)
XLA Modules:
  0.0 108.5 jit_solution(2783055264976132553)
XLA Ops:
  0.0 1.6 %copy.10.window_ref = s32[32,12,2]{2,1,0:T(8,128)} copy(s32[32,12,2]{0,2,1:T(2,128)} %param.17) | data formatting | bytes 6144 | tf_op args[8]
  1.6 105.2 %shard_map.91 = bf16[1,128,1536]{2,1,0:T(8,128)(2,1)} custom-call(bf16[1,128,1536]{2,1,0:T(8,128)(2,1)} %q_hbm.1, bf16[1,128,1536]{2,1,0:T(8,128)(2,1)} %k_hbm.1, bf16[1,128,1536]{2,1,0:T(8,128)(2,1)} %v_hbm.1, bf16[1,1536,1536]{2,1,0:T(8,128)(2,1)} %wq_hbm.1, bf16[1,1536,1536]{2,1,0:T(8,128)(2,1)} %wk_hbm.1, bf16[1,1536,1536]{2,1,0:T(8,128)(2,1)} %wv_hbm.1, ...), custom_call_target="tpu_custom_call" | custom-call | tf_op jit(solution)/shard_map/pallas_call | solution.py:349
  106.8 1.8 %copy.12 = bf16[1,128,1536]{2,1,0:T(8,128)(2,1)} copy(bf16[1,128,1536]{2,1,0:T(8,128)(2,1)} %shard_map.91) | data formatting | bytes 786432

commit v4 on v2

--- a/solution.py
+++ b/solution.py
@@ -10,6 +10,8 @@
 HEAD_DIM = 128
 COLUMN = 4
 CHUNK = 256
+LAG = 2
+GROUPS = 3
 MESH = pl.DeviceIdType.MESH
 F32 = jnp.float32
 BF16 = jnp.bfloat16
@@ -26,9 +28,9 @@
 
 def relay_kernel(
     sections, tiles, heads, tile,
-    q_hbm, k_hbm, v_hbm, wq_hbm, wk_hbm, wv_hbm, wo_hbm, up_hbm, window_ref,
+    q_hbm, k_hbm, v_hbm, wq_hbm, wk_hbm, wv_hbm, wo_hbm, up_hbm, window_hbm,
     out_ref,
-    qx, kx, vx, wq, wk, wv, wo, inx, acc, dx, prob, prob_t, mean_v, lsx, dlt, grad, res, stat,
+    qx, kx, vx, wq, wk, wv, wo, inx, acc, dx, prob, prob_t, mean_v, lsx, dlt, grad, res, stat, window, flags,
     load_sem, wsem, up_sem,
     kv_send, kv_recv, ls_send, ls_recv, hop_send, hop_recv, fwd_send, fwd_recv, dl_send, dl_recv,
 ):
@@ -66,6 +68,8 @@
         pltpu.make_async_copy(source.at[0], target.at[own], load_sem.at[n])
         for n, (source, target) in enumerate(((k_hbm, kx), (v_hbm, vx), (q_hbm, qx)))
     ]
+    window_load = pltpu.make_async_copy(window_hbm, window, load_sem.at[3])
+    window_load.start()
     for copy in own_loads:
         copy.start()
     weight_loads = [
@@ -97,9 +101,9 @@
         one(has_left) + one(has_right) + one(sends_on) + one(jnp.logical_not(is_first)),
     )
 
-    def exchange(ordinal, side, target, rows, source, into):
+    def exchange(ordinal, side, target, rows, cols, source, into):
         return pltpu.make_async_remote_copy(
-            src_ref=source, dst_ref=into.at[rows],
+            src_ref=source.at[0, :, cols], dst_ref=into.at[rows, cols],
             send_sem=kv_send.at[ordinal, side], recv_sem=kv_recv.at[ordinal, side],
             device_id=target, device_id_type=MESH,
         )
@@ -117,16 +121,21 @@
             def _(side=side, target=target, rows=rows):
                 forward_chunk(n, side, target, rows).start()
 
-    statics = ((0, k_hbm, kx), (1, v_hbm, vx), (2, q_hbm, qx))
-
-    def start_static(ordinal, source, into):
+    group = heads // GROUPS
+    every = pl.ds(0, width)
+    statics = [(0, every, k_hbm, kx), (1, every, v_hbm, vx)] + [
+        (2 + g, pl.ds(g * group * HEAD_DIM, group * HEAD_DIM), q_hbm, qx) for g in range(GROUPS)
+    ]
+
+    def start_static(ordinal):
+        _, cols, source, into = statics[ordinal]
         for side, present, target, rows in sides:
             @pl.when(present)
             def _(side=side, target=target, rows=rows):
-                exchange(ordinal, side, target, rows, source.at[0], into).start()
-
-    start_static(*statics[0])
-    start_static(*statics[1])
+                exchange(ordinal, side, target, rows, cols, source, into).start()
+
+    start_static(0)
+    start_static(1)
 
     @pl.when(is_first)
     def _():
@@ -136,14 +145,13 @@
             ).wait()
             forward_all(n)
 
-    start_static(*statics[2])
-
-    def wait_static(ordinal, into):
+    def wait_static(ordinal):
+        _, cols, _, into = statics[ordinal]
         for side, present, rows in here:
             @pl.when(present)
             def _(side=side, rows=rows):
                 pltpu.make_async_remote_copy(
-                    src_ref=into.at[own], dst_ref=into.at[rows],
+                    src_ref=into.at[own, cols], dst_ref=into.at[rows, cols],
                     send_sem=kv_send.at[ordinal, 1 - side], recv_sem=kv_recv.at[ordinal, 1 - side],
                     device_id={"seq": me}, device_id_type=MESH,
                 ).wait_recv()
@@ -168,35 +176,65 @@
             return pl.ds(h * HEAD_DIM, HEAD_DIM)
         return pl.ds(pl.multiple_of(h * HEAD_DIM, HEAD_DIM), HEAD_DIM)
 
-    def flag(index, h, which):
-        return window_ref[index, pl.ds(h, 1), which:which + 1]
+    def flag(kind, h):
+        return flags[kind, pl.ds(h, 1), 0:1]
 
     before = jnp.maximum(me - 1, 0)
     after = jnp.minimum(me + 1, tiles - 1)
 
-    for copy in own_loads[:2]:
+    def accumulate(n, row_sets):
+        rows_in = [inx[n, rows, :] for rows in row_sets]
+        incoming = rows_in[0] if len(rows_in) == 1 else jnp.concatenate(rows_in, axis=0)
+        for m in range(width // CHUNK):
+            out_cols = pl.ds(m * CHUNK, CHUNK)
+            product = nt(incoming, wo[out_cols, pl.ds(n * CHUNK, CHUNK)])
+            for i, rows in enumerate(row_sets):
+                part = product[i * tile:(i + 1) * tile]
+                if n > 0:
+                    part = part + acc[rows, out_cols]
+                if n == chunks - 1:
+                    dx[rows, out_cols] = part.astype(BF16)
+                else:
+                    acc[rows, out_cols] = part
+
+    @pl.when(is_first)
+    def _():
+        weight_loads[0].wait()
+        for n in range(chunks):
+            accumulate(n, (own,))
+
+    window_load.wait()
+    places = lax.broadcasted_iota(jnp.int32, (heads, tiles), 1)
+    for kind, (index, which) in enumerate(((me, 0), (me, 1), (before, 1), (after, 0))):
+        picked = jnp.where(places == index, window[:, which, :], 0).astype(F32)
+        picked = jnp.sum(picked, axis=1, keepdims=True)
+        flags[kind, 0:heads, :] = jnp.broadcast_to(picked, (heads, 128))
+
+    for copy in own_loads:
         copy.wait()
-    wait_static(0, kx)
-    wait_static(1, vx)
+    wait_static(0)
 
     def forward_head(h, table):
         cols = head_cols(h)
         scores = scaling * nt(qx[own, cols], kx[:, cols])
-        left = jnp.where(flag(me, h, 0) > 0, scores[:, :tile], LOW)
-        right = jnp.where(flag(me, h, 1) > 0, scores[:, 2 * tile:], LOW)
+        left = jnp.where(flag(0, h) > 0, scores[:, :tile], LOW)
+        right = jnp.where(flag(1, h) > 0, scores[:, 2 * tile:], LOW)
         scores = jnp.concatenate([left, scores[:, tile:2 * tile], right], axis=1)
         top = jnp.max(scores, axis=1, keepdims=True)
         powers = jnp.exp(scores - top)
         total = jnp.sum(powers, axis=1, keepdims=True)
-        weights = powers * (1.0 / total)
-        prob[h] = weights
+        prob[h] = powers * (1.0 / total)
+        return jnp.where(lanes == h, top + jnp.log(total), table)
+
+    def mean_head(h, carry):
+        cols = head_cols(h)
+        weights = prob[h]
         high = weights.astype(BF16)
         rest = (weights - high.astype(F32)).astype(BF16)
         values = vx[:, cols]
         mean_v[:, cols] = nn(high, values) + nn(rest, values)
-        return jnp.where(lanes == h, top + jnp.log(total), table)
-
-    own_loads[2].wait()
+        return carry
+
     table = lax.fori_loop(0, heads, forward_head, jnp.zeros((tile, 128), F32), unroll=4)
     stat[...] = table.T
     lsx[:, own] = stat[0:16, :]
@@ -205,24 +243,48 @@
         def _(side=side, target=target, rows=rows):
             small_copy(lsx.at[:, own], lsx, rows, side, ls_send, ls_recv, target).start()
 
+    start_static(2)
+    wait_static(1)
+    lax.fori_loop(0, heads, mean_head, 0, unroll=4)
+
+    def delta_head(h, table):
+        cols = head_cols(h)
+        delta = jnp.sum(dx[own, cols].astype(F32) * mean_v[:, cols], axis=1, keepdims=True)
+        return jnp.where(lanes == h, delta, table)
+
+    def send_delta():
+        table = jnp.zeros((tile, 128), F32)
+        for h in range(heads):
+            table = delta_head(h, table)
+        stat[...] = table.T
+        dlt[:, own] = stat[0:16, :]
+        for side, present, target, rows in sides:
+            @pl.when(present)
+            def _(side=side, target=target, rows=rows):
+                small_copy(dlt.at[:, own], dlt, rows, side, dl_send, dl_recv, target).start()
+
+    pl.when(is_first)(send_delta)
+    for ordinal in range(3, 2 + GROUPS):
+        start_static(ordinal)
+
     def transposed_head(h, carry):
         cols = head_cols(h)
         scores = scaling * nt(kx[own, cols], qx[:, cols]) - lsx[pl.ds(h, 1), :]
-        left_flag = jnp.logical_and(flag(before, h, 1) > 0, me > 0)
-        right_flag = jnp.logical_and(flag(after, h, 0) > 0, me < tiles - 1)
+        left_flag = jnp.logical_and(flag(2, h) > 0, me > 0)
+        right_flag = jnp.logical_and(flag(3, h) > 0, me < tiles - 1)
         left = jnp.where(left_flag, scores[:, :tile], LOW)
         right = jnp.where(right_flag, scores[:, 2 * tile:], LOW)
         scores = jnp.concatenate([left, scores[:, tile:2 * tile], right], axis=1)
         prob_t[h] = jnp.exp(scores)
         return carry
 
-    def transposed_all():
-        wait_static(2, qx)
+    @pl.when(jnp.logical_not(is_first))
+    def _():
+        for g in range(GROUPS):
+            wait_static(2 + g)
         wait_small(lsx, ls_send, ls_recv)
         lax.fori_loop(0, heads, transposed_head, 0, unroll=4)
-
-    pl.when(jnp.logical_not(is_first))(transposed_all)
-    weight_loads[0].wait()
+        weight_loads[0].wait()
 
     def hop_copy(n):
         return pltpu.make_async_remote_copy(
@@ -237,46 +299,21 @@
             def _(side=side, rows=rows):
                 forward_chunk(n, 1 - side, {"seq": me}, rows).wait_recv()
 
-    def accumulate(n):
-        k_cols = pl.ds(n * CHUNK, CHUNK)
-        last = n == chunks - 1
-
-        for m in range(width // CHUNK):
-            out_cols = pl.ds(m * CHUNK, CHUNK)
-            part = nt(inx[n], wo[out_cols, k_cols])
-            if n > 0:
-                part = part + acc[:, out_cols]
-            if last:
-                dx[:, out_cols] = part.astype(BF16)
-            else:
-                acc[:, out_cols] = part
+    def accumulate_halo(n):
+        wait_forwarded(n)
+        accumulate(n, (low_rows, high_rows))
 
     for n in range(chunks):
+        if n >= LAG:
+            accumulate_halo(n - LAG)
+
         @pl.when(jnp.logical_not(is_first))
         def _(n=n):
             hop_copy(n).wait_recv()
             forward_all(n)
-        if n > 0:
-            wait_forwarded(n - 1)
-            accumulate(n - 1)
-    wait_forwarded(chunks - 1)
-    accumulate(chunks - 1)
-    pl.when(is_first)(transposed_all)
-
-    def delta_head(h, table):
-        cols = head_cols(h)
-        delta = jnp.sum(dx[own, cols].astype(F32) * mean_v[:, cols], axis=1, keepdims=True)
-        return jnp.where(lanes == h, delta, table)
-
-    table = jnp.zeros((tile, 128), F32)
-    for h in range(heads):
-        table = delta_head(h, table)
-    stat[...] = table.T
-    dlt[:, own] = stat[0:16, :]
-    for side, present, target, rows in sides:
-        @pl.when(present)
-        def _(side=side, target=target, rows=rows):
-            small_copy(dlt.at[:, own], dlt, rows, side, dl_send, dl_recv, target).start()
+            accumulate(n, (own,))
+
+    pl.when(jnp.logical_not(is_first))(send_delta)
 
     def query_head(h):
         cols = head_cols(h)
@@ -284,19 +321,35 @@
         delta = jnp.sum(d_own.astype(F32) * mean_v[:, cols], axis=1, keepdims=True)
         change = (prob[h] * (nt(d_own, vx[:, cols]) - delta)).astype(BF16)
         grad[0, :, cols] = (scaling * nn(change, kx[:, cols])).astype(BF16)
-        grad[2, :, cols] = nn(prob_t[h].astype(BF16), dx[:, cols]).astype(BF16)
 
     for h in range(heads):
         query_head(h)
-    wait_small(dlt, dl_send, dl_recv)
+    for n in range(chunks - LAG, chunks):
+        accumulate_halo(n)
 
     def key_head(h):
         cols = head_cols(h)
+        grad[2, :, cols] = nn(prob_t[h].astype(BF16), dx[:, cols]).astype(BF16)
         change = (prob_t[h] * (nt(vx[own, cols], dx[:, cols]) - dlt[pl.ds(h, 1), :])).astype(BF16)
         grad[1, :, cols] = (scaling * nn(change, qx[:, cols])).astype(BF16)
 
-    for h in range(heads):
-        key_head(h)
+    @pl.when(is_first)
+    def _():
+        wait_small(lsx, ls_send, ls_recv)
+        wait_small(dlt, dl_send, dl_recv)
+        for g in range(GROUPS):
+            wait_static(2 + g)
+            for h in range(g * group, (g + 1) * group):
+                transposed_head(h, 0)
+            for h in range(g * group, (g + 1) * group):
+                key_head(h)
+
+    @pl.when(jnp.logical_not(is_first))
+    def _():
+        wait_small(dlt, dl_send, dl_recv)
+        for h in range(heads):
+            key_head(h)
+
     for copy in weight_loads[1:]:
         copy.wait()
 
@@ -315,8 +368,8 @@
     for side, present, target, rows in sides:
         @pl.when(present)
         def _(side=side, target=target, rows=rows):
-            for ordinal, source, into in statics:
-                exchange(ordinal, side, target, rows, source.at[0], into).wait_send()
+            for ordinal, cols, source, into in statics:
+                exchange(ordinal, side, target, rows, cols, source, into).wait_send()
             small_copy(lsx.at[:, own], lsx, rows, side, ls_send, ls_recv, target).wait_send()
             small_copy(dlt.at[:, own], dlt, rows, side, dl_send, dl_recv, target).wait_send()
             for n in range(chunks):
@@ -342,7 +395,7 @@
     return pl.pallas_call(
         functools.partial(relay_kernel, sections, tiles, heads, tile),
         out_shape=jax.ShapeDtypeStruct((1, tile, model), BF16),
-        in_specs=[hbm] * 8 + [vmem],
+        in_specs=[hbm] * 9,
         out_specs=vmem,
         scratch_shapes=[
             pltpu.VMEM((3 * tile, width), BF16),
@@ -363,15 +416,17 @@
             pltpu.VMEM((3, tile, width), BF16),
             pltpu.VMEM((chunks, tile, CHUNK), BF16),
             pltpu.VMEM((128, tile), F32),
-            dma((3,)), dma((4,)), dma((chunks,)),
-            dma((3, 2)), dma((3, 2)), dma((2,)), dma((2,)),
+            pltpu.VMEM((heads, 2, tiles), jnp.int32),
+            pltpu.VMEM((4, 16, 128), F32),
+            dma((4,)), dma((4,)), dma((chunks,)),
+            dma((2 + GROUPS, 2)), dma((2 + GROUPS, 2)), dma((2,)), dma((2,)),
             dma((chunks,)), dma((chunks,)), dma((chunks, 2)), dma((chunks, 2)),
             dma((2,)), dma((2,)),
         ],
         compiler_params=pltpu.CompilerParams(
             collective_id=0, has_side_effects=True, vmem_limit_bytes=60 * 1024 * 1024
         ),
-    )(q, k, v, wq, wk, wv, wo, upstream, window)
+    )(q, k, v, wq, wk, wv, wo, upstream, jnp.transpose(window, (1, 2, 0)))
 
 
 def solution(mesh):

time: 121 us -> 102 us (0.84); the launches traced: 119 us -> 101 us
  Pallas kernels: 116 us -> 99.7 us
  local copies, waits for them, and re-layouts: 3.35 us -> 1.77 us
    pallas_call x1, Pallas kernels: 116 us -> 99.7 us  [body(): pl.pallas_call(functools.partial(relay_kernel, sections, tiles, heads, ti...]
    unnamed x2 -> x1, local copies, waits for them, and re-layouts: 3.35 us -> 1.77 us
where the time goes in v4:
time: 102 us; the launch traced here: 101 us
  Pallas kernels  99.7 us (98%)
  local copies, waits for them, and re-layouts  1.77 us (2%)
    pallas_call x1, Pallas kernels, body(): pl.pallas_call(functools.partial(relay_kernel, sections, tiles, heads, ti...  99.7 us

profile of v4, /device:TPU:57, one launch (start us, length us, event | category | flops | bytes accessed | tf_op | source)
XLA Modules:
  0.0 101.5 jit_solution(7262742190104850620)
XLA Ops:
  0.0 99.7 %shard_map.91 = bf16[1,128,1536]{2,1,0:T(8,128)(2,1)} custom-call(bf16[1,128,1536]{2,1,0:T(8,128)(2,1)} %q_hbm.1, bf16[1,128,1536]{2,1,0:T(8,128)(2,1)} %k_hbm.1, bf16[1,128,1536]{2,1,0:T(8,128)(2,1)} %v_hbm.1, bf16[1,1536,1536]{2,1,0:T(8,128)(2,1)} %wq_hbm.1, bf16[1,1536,1536]{2,1,0:T(8,128)(2,1)} %wk_hbm.1, bf16[1,1536,1536]{2,1,0:T(8,128)(2,1)} %wv_hbm.1, ...), custom_call_target="tpu_custom_call" | custom-call | tf_op jit(solution)/shard_map/pallas_call | solution.py:395
  99.7 1.8 %copy.11 = bf16[1,128,1536]{2,1,0:T(8,128)(2,1)} copy(bf16[1,128,1536]{2,1,0:T(8,128)(2,1)} %shard_map.91) | data formatting | bytes 786432

commit v5 on v4

--- a/solution.py
+++ b/solution.py
@@ -30,7 +30,7 @@
     sections, tiles, heads, tile,
     q_hbm, k_hbm, v_hbm, wq_hbm, wk_hbm, wv_hbm, wo_hbm, up_hbm, window_hbm,
     out_ref,
-    qx, kx, vx, wq, wk, wv, wo, inx, acc, dx, prob, prob_t, mean_v, lsx, dlt, grad, res, stat, window, flags,
+    qx, kx, vx, wq, wk, wv, wo, inx, acc, dx, prob, prob_t, mean_v, lsx, dlt, grad, res, stat, window, flags, part_k, part_v,
     load_sem, wsem, up_sem,
     kv_send, kv_recv, ls_send, ls_recv, hop_send, hop_recv, fwd_send, fwd_recv, dl_send, dl_recv,
 ):
@@ -324,6 +324,30 @@
 
     for h in range(heads):
         query_head(h)
+
+    def key_own(h):
+        cols = head_cols(h)
+        share = prob_t[h, :, own]
+        d_own = dx[own, cols]
+        part_v[:, cols] = nn(share.astype(BF16), d_own)
+        change = (share * (nt(vx[own, cols], d_own) - dlt[pl.ds(h, 1), own])).astype(BF16)
+        part_k[:, cols] = nn(change, qx[own, cols])
+
+    def key_halo(h):
+        cols = head_cols(h)
+        outer = lambda ref: jnp.concatenate([ref[low_rows, cols], ref[high_rows, cols]], axis=0)
+        share = jnp.concatenate([prob_t[h, :, low_rows], prob_t[h, :, high_rows]], axis=1)
+        delta = jnp.concatenate([dlt[pl.ds(h, 1), low_rows], dlt[pl.ds(h, 1), high_rows]], axis=1)
+        d_outer = outer(dx)
+        grad[2, :, cols] = (part_v[:, cols] + nn(share.astype(BF16), d_outer)).astype(BF16)
+        change = (share * (nt(vx[own, cols], d_outer) - delta)).astype(BF16)
+        grad[1, :, cols] = (scaling * (part_k[:, cols] + nn(change, outer(qx)))).astype(BF16)
+
+    @pl.when(jnp.logical_not(is_first))
+    def _():
+        for h in range(heads):
+            key_own(h)
+
     for n in range(chunks - LAG, chunks):
         accumulate_halo(n)
 
@@ -348,7 +372,7 @@
     def _():
         wait_small(dlt, dl_send, dl_recv)
         for h in range(heads):
-            key_head(h)
+            key_halo(h)
 
     for copy in weight_loads[1:]:
         copy.wait()
@@ -418,6 +442,8 @@
             pltpu.VMEM((128, tile), F32),
             pltpu.VMEM((heads, 2, tiles), jnp.int32),
             pltpu.VMEM((4, 16, 128), F32),
+            pltpu.VMEM((tile, width), F32),
+            pltpu.VMEM((tile, width), F32),
             dma((4,)), dma((4,)), dma((chunks,)),
             dma((2 + GROUPS, 2)), dma((2 + GROUPS, 2)), dma((2,)), dma((2,)),
             dma((chunks,)), dma((chunks,)), dma((chunks, 2)), dma((chunks, 2)),

time: 102 us -> 101 us (level)
  no operation moved by 1% of the time
where the time goes in v5:
time: 101 us
  Pallas kernels  99 us (98%)
  local copies, waits for them, and re-layouts  1.77 us (2%)
    pallas_call x1, Pallas kernels, body(): pl.pallas_call(functools.partial(relay_kernel, sections, tiles, heads, ti...  99 us

profile of v5, /device:TPU:57, one launch (start us, length us, event | category | flops | bytes accessed | tf_op | source)
XLA Modules:
  0.0 100.8 jit_solution(15615866619673033822)
XLA Ops:
  0.0 99.0 %shard_map.91 = bf16[1,128,1536]{2,1,0:T(8,128)(2,1)} custom-call(bf16[1,128,1536]{2,1,0:T(8,128)(2,1)} %q_hbm.1, bf16[1,128,1536]{2,1,0:T(8,128)(2,1)} %k_hbm.1, bf16[1,128,1536]{2,1,0:T(8,128)(2,1)} %v_hbm.1, bf16[1,1536,1536]{2,1,0:T(8,128)(2,1)} %wq_hbm.1, bf16[1,1536,1536]{2,1,0:T(8,128)(2,1)} %wk_hbm.1, bf16[1,1536,1536]{2,1,0:T(8,128)(2,1)} %wv_hbm.1, ...), custom_call_target="tpu_custom_call" | custom-call | tf_op jit(solution)/shard_map/pallas_call | solution.py:419
  99.0 1.8 %copy.11 = bf16[1,128,1536]{2,1,0:T(8,128)(2,1)} copy(bf16[1,128,1536]{2,1,0:T(8,128)(2,1)} %shard_map.91) | data formatting | bytes 786432

commit v6 on v5

--- a/solution.py
+++ b/solution.py
@@ -304,14 +304,14 @@
         accumulate(n, (low_rows, high_rows))
 
     for n in range(chunks):
-        if n >= LAG:
-            accumulate_halo(n - LAG)
-
         @pl.when(jnp.logical_not(is_first))
         def _(n=n):
             hop_copy(n).wait_recv()
             forward_all(n)
             accumulate(n, (own,))
+
+        if LAG <= n < chunks - 1:
+            accumulate_halo(n - LAG)
 
     pl.when(jnp.logical_not(is_first))(send_delta)
 
@@ -348,7 +348,7 @@
         for h in range(heads):
             key_own(h)
 
-    for n in range(chunks - LAG, chunks):
+    for n in range(chunks - 1 - LAG, chunks):
         accumulate_halo(n)
 
     def key_head(h):

time: 101 us -> 92.6 us (0.917)
  Pallas kernels: 99 us -> 90.5 us
    pallas_call x1, Pallas kernels: 99 us -> 90.5 us  [body(): pl.pallas_call(functools.partial(relay_kernel, sections, tiles, heads, ti...]
where the time goes in v6:
time: 92.6 us; the launch traced here: 92.2 us
  Pallas kernels  90.5 us (98%)
  local copies, waits for them, and re-layouts  1.77 us (2%)
    pallas_call x1, Pallas kernels, body(): pl.pallas_call(functools.partial(relay_kernel, sections, tiles, heads, ti...  90.5 us

profile of v6, /device:TPU:57, one launch (start us, length us, event | category | flops | bytes accessed | tf_op | source)
XLA Modules:
  0.0 92.2 jit_solution(6428300710594465451)
XLA Ops:
  0.0 90.5 %shard_map.91 = bf16[1,128,1536]{2,1,0:T(8,128)(2,1)} custom-call(bf16[1,128,1536]{2,1,0:T(8,128)(2,1)} %q_hbm.1, bf16[1,128,1536]{2,1,0:T(8,128)(2,1)} %k_hbm.1, bf16[1,128,1536]{2,1,0:T(8,128)(2,1)} %v_hbm.1, bf16[1,1536,1536]{2,1,0:T(8,128)(2,1)} %wq_hbm.1, bf16[1,1536,1536]{2,1,0:T(8,128)(2,1)} %wk_hbm.1, bf16[1,1536,1536]{2,1,0:T(8,128)(2,1)} %wv_hbm.1, ...), custom_call_target="tpu_custom_call" | custom-call | tf_op jit(solution)/shard_map/pallas_call | solution.py:419
  90.5 1.8 %copy.11 = bf16[1,128,1536]{2,1,0:T(8,128)(2,1)} copy(bf16[1,128,1536]{2,1,0:T(8,128)(2,1)} %shard_map.91) | data formatting | bytes 786432
